TPU v7x, 32 devices: a whole 2x2x4 slice. The times are simulated.
32 devices in a mesh: seq: 8 (over z, x), head: 2 (over y), dp: 2 (over core).
Axes of the slice: x: 2, y: 2, z: 4, core: 2. Of those that a mesh axis runs over, the one named last changes fastest.
Arguments:
- queries: bfloat16 [2, 2048, 1024], P('dp', 'seq', 'head'), may hold values from -6 to 6
- key_rows: bfloat16 [2, 2048, 1024], P('dp', 'seq', 'head'), may hold values from -6 to 6
- value_rows: bfloat16 [2, 2048, 1024], P('dp', 'seq', 'head'), may hold values from -140 to 140
- stretch_doc: int32 [2, 8], P('dp', 'seq'), may hold values from 0 to 3, never falling along the last dimension, each value on 1 to 4 neighbouring positions
- head_gain: float32 [8, 128], P('head'), may hold values from 0.1 to 1.9
- w_out: bfloat16 [1024, 2048], P('head'), may hold values from -0.1875 to 0.1875
- cotangent: bfloat16 [2, 2048, 2048], P('dp', 'seq'), may hold values from -40 to 40
Outputs:
- layer_out: bfloat16 [2, 2048, 2048], P('dp', ('seq', 'head'))
- query_grad: bfloat16 [2, 2048, 1024], P('dp', 'seq', 'head')
- key_grad: bfloat16 [2, 2048, 1024], P('dp', 'seq', 'head')
- value_grad: bfloat16 [2, 2048, 1024], P('dp', 'seq', 'head')
- gain_grad: float32 [8, 128], P('head')
Inputs may be any that keep to these rules, and one draw needn't show every extreme that they name: `stretch_doc`: document numbers never fall along a sequence; each document spans 1 to 4 whole stretches, and one spans exactly that many.
All inputs are finite; a program needn't handle non-finite values.
Results may differ from a plain program's by a relative error of at most 0.0055.
Values may be sent and summed in bfloat16 or wider, within the bound.
No kernel may reach another device: no remote copies, remote signals or barrier semaphores. Data moves between devices by JAX's collectives and lax.ppermute only.
A program may use at most 64 MiB of HBM per device.

v0:
```python
import math
import jax
import jax.numpy as jnp
from jax import lax
from jax.sharding import PartitionSpec as P

epsilon = 1e-05
highest = lax.Precision.HIGHEST


def shifted(block, axis, distance):
    devices = range(lax.axis_size(axis))
    route = [(i - distance, i) for i in devices if i - distance in devices]
    return lax.ppermute(block, axis, route)


def link_docs(earlier, following):
    sum_early, doc_early = earlier
    sum_late, doc_late = following
    merged = jnp.where(doc_early[0] == doc_late[0], sum_late + sum_early, sum_late)
    running = jnp.where(doc_late[0] < 0.5, sum_early, merged)
    return (running, jnp.where(doc_late < 0.5, doc_early, doc_late))


def double_chain(start, mover, seq_size):
    current = mover(start, 1)
    reach = 1
    while reach < seq_size - 1:
        current = link_docs(mover(current, reach), current)
        reach = reach * 2
    return current


def on_device(queries, key_rows, value_rows, stretch_doc, head_gain, w_out, cotangent):
    token_count = queries.shape[1]
    local_width = queries.shape[2]
    head_count = head_gain.shape[0]
    head_dim = head_gain.shape[1]
    stretches = stretch_doc.shape[1]
    stretch_len = token_count // stretches
    seq_size = lax.axis_size("seq")
    blocks = (stretches, stretch_len, head_count, head_dim)
    query_blk = queries[0].reshape(blocks)
    key_blk = key_rows[0].reshape(blocks)
    value_blk = value_rows[0].reshape(blocks)
    doc_ids = stretch_doc[0]
    doc_float = doc_ids.astype(jnp.float32) + 1.0
    stretch_order = jnp.arange(stretches)
    same_doc = doc_ids[:, None] == doc_ids[None, :]
    before_mask = jnp.where(
        same_doc & (stretch_order[None, :] < stretch_order[:, None]), 1.0, 0.0
    ).astype(jnp.float32)
    after_mask = jnp.where(
        same_doc & (stretch_order[None, :] > stretch_order[:, None]), 1.0, 0.0
    ).astype(jnp.float32)
    positions = jnp.arange(stretch_len)
    causal = positions[:, None] >= positions[None, :]

    def move_forward(pair, distance):
        return shifted((pair[0], pair[1]), "seq", distance)

    def move_backward(pair, distance):
        return shifted((pair[0], pair[1]), "seq", -distance)

    kv_sum = jnp.einsum("cshd,cshe->chde", key_blk, value_blk, preferred_element_type=jnp.float32)
    last_pick = jnp.where(doc_float == doc_float[0], 1.0, 0.0).astype(jnp.float32)
    own_state = jnp.einsum("c,chde->hde", last_pick, kv_sum, precision=highest)
    incoming, incoming_doc = double_chain((own_state, doc_float), move_forward, seq_size)
    take_in = jnp.where(doc_float == incoming_doc[0], 1.0, 0.0).astype(jnp.float32)
    states = (
        jnp.einsum("cj,jhde->chde", before_mask, kv_sum, precision=highest)
        + take_in[:, None, None, None] * incoming
    )
    scores = jnp.einsum("cthd,cshd->chts", query_blk, key_blk, preferred_element_type=jnp.float32)
    attn_weights = jnp.where(causal, scores, 0.0).astype(jnp.bfloat16)
    within = jnp.einsum(
        "chts,cshe->cthe", attn_weights, value_blk, preferred_element_type=jnp.float32
    )
    query_f = query_blk.astype(jnp.float32)
    carried = jnp.einsum("cthd,chde->cthe", query_f, states, precision=highest)
    attended = within + carried
    inv_rms = lax.rsqrt(jnp.mean(attended * attended, axis=-1, keepdims=True) + epsilon)
    unit_rows = attended * inv_rms
    normed_rows = (unit_rows * head_gain).astype(jnp.bfloat16).reshape(token_count, local_width)
    exchanged = lax.all_to_all(normed_rows, "head", split_axis=0, concat_axis=1, tiled=True)
    summed = jnp.dot(
        exchanged,
        lax.all_gather(w_out, "head", axis=0, tiled=True),
        preferred_element_type=jnp.float32,
    )
    layer_out = summed.astype(jnp.bfloat16)[None]
    grad_normed = jnp.einsum(
        "tm,fm->tf", cotangent[0], w_out, preferred_element_type=jnp.float32
    ).reshape(blocks)
    gain_part = jnp.sum(grad_normed * unit_rows, axis=(0, 1))
    total_tokens = seq_size * lax.axis_size("dp") * token_count
    gain_grad = lax.psum(gain_part, ("seq", "dp")) / math.sqrt(total_tokens)
    scaled = grad_normed * head_gain
    grad_attended = inv_rms * (
        scaled - unit_rows * jnp.mean(scaled * unit_rows, axis=-1, keepdims=True)
    )
    grad_bf = grad_attended.astype(jnp.bfloat16)
    query_term = jnp.einsum(
        "cthd,cthe->chde", query_blk, grad_bf, preferred_element_type=jnp.float32
    )
    first_pick = jnp.where(doc_float == doc_float[0], 1.0, 0.0).astype(jnp.float32)
    own_grad = jnp.einsum("c,chde->hde", first_pick, query_term, precision=highest)
    incoming_grad, grad_doc = double_chain((own_grad, doc_float), move_backward, seq_size)
    take_back = jnp.where(doc_float == grad_doc[0], 1.0, 0.0).astype(jnp.float32)
    grad_states = (
        jnp.einsum("cj,jhde->chde", after_mask, query_term, precision=highest)
        + take_back[:, None, None, None] * incoming_grad
    )
    grad_scores = jnp.einsum(
        "cthe,cshe->chts", grad_bf, value_blk, preferred_element_type=jnp.float32
    )
    grad_weights = jnp.where(causal, grad_scores, 0.0).astype(jnp.bfloat16)
    grad_f = grad_bf.astype(jnp.float32)
    query_grad = jnp.einsum(
        "chts,cshd->cthd", grad_weights, key_blk, preferred_element_type=jnp.float32
    ) + jnp.einsum("cthe,chde->cthd", grad_f, states, precision=highest)
    key_grad = jnp.einsum(
        "chts,cthd->cshd", grad_weights, query_blk, preferred_element_type=jnp.float32
    ) + jnp.einsum("cshe,chde->cshd", value_blk.astype(jnp.float32), grad_states, precision=highest)
    value_grad = jnp.einsum(
        "chts,cthe->cshe", attn_weights, grad_bf, preferred_element_type=jnp.float32
    ) + jnp.einsum("cshd,chde->cshe", key_blk.astype(jnp.float32), grad_states, precision=highest)
    out_shape = (1, token_count, local_width)
    return (
        layer_out,
        query_grad.astype(jnp.bfloat16).reshape(out_shape),
        key_grad.astype(jnp.bfloat16).reshape(out_shape),
        value_grad.astype(jnp.bfloat16).reshape(out_shape),
        gain_grad,
    )


def solution(mesh):
    return jax.shard_map(
        on_device,
        mesh=mesh,
        in_specs=(
            P("dp", "seq", "head"),
            P("dp", "seq", "head"),
            P("dp", "seq", "head"),
            P("dp", "seq"),
            P("head", None),
            P("head", None),
            P("dp", "seq", None),
        ),
        out_specs=(
            P("dp", ("seq", "head"), None),
            P("dp", "seq", "head"),
            P("dp", "seq", "head"),
            P("dp", "seq", "head"),
            P("head", None),
        ),
        check_vma=False,
    )
```

profile of v0, /device:TPU:7, one launch (start us, length us, event | category | flops | bytes accessed | tf_op | source)
XLA Modules:
  0.0 170.7 jit_solution(11719621536188737796)
XLA Ops:
  7.2 0.0 copy-start
  7.2 0.0 all-gather.2.cloned.1.call-start
  8.0 1.0 reshape.195
  9.0 0.2 copy.35
  9.2 1.0 reshape.196
  10.2 0.2 broadcast_multiply_fusion
  10.5 3.2 %collective-permute-start.4 = (f32[4,128,128]{2,1,0:T(8,128)S(1)}, f32[4,128,128]{2,1,0:T(8,128)S(1)}, u32[]{:S(2)}, u32[]{:S(2)}) collective-permute-start(f32[4,128,128]{2,1,0:T(8,128)S(1)} %get-tuple-element.19), channel_id=1, source_target_pairs={{0,4},{4,8},{8,12},{12,16},{16,20},{20,24},{24,28},{1,5},{5,9},{9,... | collective-permute-start | bytes 786440 | tf_op jit(solution)/shard_map/ppermute | solution.py:14
  13.6 5.9 %collective-permute-done.4 = f32[4,128,128]{2,1,0:T(8,128)S(1)} collective-permute-done((f32[4,128,128]{2,1,0:T(8,128)S(1)}, f32[4,128,128]{2,1,0:T(8,128)S(1)}, u32[]{:S(2)}, u32[]{:S(2)}) %collective-permute-start.4) | collective-permute-done | bytes 262176 | tf_op jit(solution)/shard_map/ppermute | solution.py:14
  19.5 4.0 %collective-permute-start.5 = (f32[4,128,128]{2,1,0:T(8,128)S(1)}, f32[4,128,128]{2,1,0:T(8,128)S(1)}, u32[]{:S(2)}, u32[]{:S(2)}) collective-permute-start(f32[4,128,128]{2,1,0:T(8,128)S(1)} %collective-permute-done.4), channel_id=1, source_target_pairs={{0,4},{4,8},{8,12},{12,16},{16,20},{20,24},{24,28},{1,5},{5,9},{9,... | collective-permute-start | bytes 786440 | tf_op jit(solution)/shard_map/ppermute | solution.py:14
  23.6 4.1 %collective-permute-start = (f32[1]{0:T(128)}, f32[1]{0:T(128)}, u32[]{:S(2)}, u32[]{:S(2)}) collective-permute-start(f32[1]{0:T(128)} %bitcast.1), channel_id=1, source_target_pairs={{0,4},{4,8},{8,12},{12,16},{16,20},{20,24},{24,28},{1,5},{5,9},{9,... | collective-permute-start | bytes 20 | tf_op jit(solution)/shard_map/ppermute | solution.py:14
  27.6 0.0 all-gather.2.cloned.1.call-update
  27.7 0.1 reshape.194
  27.8 0.4 collective-permute-done
  28.2 4.4 %collective-permute-start.1 = (f32[1]{0:T(128)}, f32[1]{0:T(128)}, u32[]{:S(2)}, u32[]{:S(2)}) collective-permute-start(f32[1]{0:T(128)} %collective-permute-done), channel_id=1, source_target_pairs={{0,4},{4,8},{8,12},{12,16},{16,20},{20,24},{24,28},{1,5},{5,9},{9,... | collective-permute-start | bytes 20 | tf_op jit(solution)/shard_map/ppermute | solution.py:14
  33.2 0.3 collective-permute-done.1
  34.8 0.0 collective-permute-done.5
  34.8 0.0 copy-start.3
  34.8 3.2 %collective-permute-start.6 = (f32[4,128,128]{2,1,0:T(8,128)S(1)}, f32[4,128,128]{2,1,0:T(8,128)S(1)}, u32[]{:S(2)}, u32[]{:S(2)}) collective-permute-start(f32[4,128,128]{2,1,0:T(8,128)S(1)} %fusion.14), channel_id=1, source_target_pairs={{0,8},{4,12},{8,16},{12,20},{16,24},{20,28},{1,9},{5,13},{9,17},{1... | collective-permute-start | bytes 786440 | tf_op jit(solution)/shard_map/ppermute | solution.py:14
  38.1 2.7 %fusion.7 = f32[256,512]{0,1:T(8,128)S(1)} fusion(bf16[512,2048]{1,0:T(8,128)(2,1)} %param.12, bf16[1,256,2048]{2,1,0:T(8,128)(2,1)S(1)} %copy-done), kind=kOutput, calls=%fused_computation.17 | convolution fusion | flops 536870912 | bytes 3670016 | tf_op jit(solution)/shard_map/tm,fm->tf/dot_general | solution.py:92
  42.0 3.9 %collective-permute-start.2 = (f32[1]{0:T(128)}, f32[1]{0:T(128)}, u32[]{:S(2)}, u32[]{:S(2)}) collective-permute-start(f32[1]{0:T(128)} %select_n.117), channel_id=1, source_target_pairs={{0,8},{4,12},{8,16},{12,20},{16,24},{20,28},{1,9},{5,13},{9,17},{1... | collective-permute-start | bytes 20 | tf_op jit(solution)/shard_map/ppermute | solution.py:14
  46.6 4.2 %collective-permute-start.7 = (f32[4,128,128]{2,1,0:T(8,128)S(1)}, f32[4,128,128]{2,1,0:T(8,128)S(1)}, u32[]{:S(2)}, u32[]{:S(2)}) collective-permute-start(f32[4,128,128]{2,1,0:T(8,128)S(1)} %fusion.13), channel_id=1, source_target_pairs={{0,16},{4,20},{8,24},{12,28},{1,17},{5,21},{9,25},{13,29},{2,18},{... | collective-permute-start | bytes 786440 | tf_op jit(solution)/shard_map/ppermute | solution.py:14
  50.8 0.3 fusion.1
  51.1 0.3 convolution_bitcast_fusion.2
  52.1 2.1 %collective-permute-start.3 = (f32[1]{0:T(128)}, f32[1]{0:T(128)}, u32[]{:S(2)}, u32[]{:S(2)}) collective-permute-start(f32[1]{0:T(128)} %select_n.118), channel_id=1, source_target_pairs={{0,16},{4,20},{8,24},{12,28},{1,17},{5,21},{9,25},{13,29},{2,18},{... | collective-permute-start | bytes 20 | tf_op jit(solution)/shard_map/ppermute | solution.py:14
  55.5 0.1 fusion.16
  55.5 0.5 multiply_reduce_fusion.2
  56.0 0.2 multiply_reduce_fusion
  56.3 0.9 fusion.19
  57.1 0.2 fusion.28
  57.4 4.2 %collective-permute-start.12 = (f32[4,128,128]{1,2,0:T(8,128)S(1)}, f32[4,128,128]{1,2,0:T(8,128)S(1)}, u32[]{:S(2)}, u32[]{:S(2)}) collective-permute-start(f32[4,128,128]{1,2,0:T(8,128)S(1)} %multiply_bitcast_fusion), channel_id=1, source_target_pairs={{4,0},{8,4},{12,8},{16,12},{20,16},{24,20},{28,24},{5,1},{9,5},{13... | collective-permute-start | bytes 786440 | tf_op jit(solution)/shard_map/ppermute | solution.py:14
  61.5 3.3 %collective-permute-start.8 = (f32[1]{0:T(128)}, f32[1]{0:T(128)}, u32[]{:S(2)}, u32[]{:S(2)}) collective-permute-start(f32[1]{0:T(128)} %bitcast.1), channel_id=1, source_target_pairs={{4,0},{8,4},{12,8},{16,12},{20,16},{24,20},{28,24},{5,1},{9,5},{13... | collective-permute-start | bytes 20 | tf_op jit(solution)/shard_map/ppermute | solution.py:14
  64.9 7.3 %collective-permute-done.8 = f32[1]{0:T(128)} collective-permute-done((f32[1]{0:T(128)}, f32[1]{0:T(128)}, u32[]{:S(2)}, u32[]{:S(2)}) %collective-permute-start.8) | collective-permute-done | bytes 36 | tf_op jit(solution)/shard_map/ppermute | solution.py:14
  72.1 1.9 %collective-permute-start.9 = (f32[1]{0:T(128)}, f32[1]{0:T(128)}, u32[]{:S(2)}, u32[]{:S(2)}) collective-permute-start(f32[1]{0:T(128)} %collective-permute-done.8), channel_id=1, source_target_pairs={{4,0},{8,4},{12,8},{16,12},{20,16},{24,20},{28,24},{5,1},{9,5},{13... | collective-permute-start | bytes 20 | tf_op jit(solution)/shard_map/ppermute | solution.py:14
  74.6 2.8 %collective-permute-done.9 = f32[1]{0:T(128)} collective-permute-done((f32[1]{0:T(128)}, f32[1]{0:T(128)}, u32[]{:S(2)}, u32[]{:S(2)}) %collective-permute-start.9) | collective-permute-done | bytes 36 | tf_op jit(solution)/shard_map/ppermute | solution.py:14
  78.7 1.3 collective-permute-start.10
  81.2 2.3 %collective-permute-done.10 = f32[1]{0:T(128)} collective-permute-done((f32[1]{0:T(128)}, f32[1]{0:T(128)}, u32[]{:S(2)}, u32[]{:S(2)}) %collective-permute-start.10) | collective-permute-done | bytes 36 | tf_op jit(solution)/shard_map/ppermute | solution.py:14
  84.1 1.3 collective-permute-start.11
  86.1 3.4 %collective-permute-done.11 = f32[1]{0:T(128)} collective-permute-done((f32[1]{0:T(128)}, f32[1]{0:T(128)}, u32[]{:S(2)}, u32[]{:S(2)}) %collective-permute-start.11) | collective-permute-done | bytes 36 | tf_op jit(solution)/shard_map/ppermute | solution.py:14
  90.8 1.9 %collective-permute-start.13 = (f32[4,128,128]{1,2,0:T(8,128)S(1)}, f32[4,128,128]{1,2,0:T(8,128)S(1)}, u32[]{:S(2)}, u32[]{:S(2)}) collective-permute-start(f32[4,128,128]{1,2,0:T(8,128)S(1)} %collective-permute-done.12), channel_id=1, source_target_pairs={{4,0},{8,4},{12,8},{16,12},{20,16},{24,20},{28,24},{5,1},{9,5},{13... | collective-permute-start | bytes 786440 | tf_op jit(solution)/shard_map/ppermute | solution.py:14
  92.7 0.3 fusion.2
  93.1 0.0 copy-start.1
  93.1 0.3 convolution_bitcast_fusion.1
  93.4 5.4 %collective-permute-done.13 = f32[4,128,128]{1,2,0:T(8,128)S(1)} collective-permute-done((f32[4,128,128]{1,2,0:T(8,128)S(1)}, f32[4,128,128]{1,2,0:T(8,128)S(1)}, u32[]{:S(2)}, u32[]{:S(2)}) %collective-permute-start.13) | collective-permute-done | bytes 262176 | tf_op jit(solution)/shard_map/ppermute | solution.py:14
  98.9 1.3 collective-permute-start.14
  100.2 0.4 fusion.4
  100.5 0.8 copy.50
  101.4 1.0 all_to_all.14
  102.4 0.7 copy.39
  103.1 3.4 %all-to-all-start = ((bf16[2,128,512]{1,2,0:T(8,128)(2,1)}), bf16[2,128,512]{1,2,0:T(8,128)(2,1)S(1)}, u32[]{:S(2)}, u32[]{:S(2)}) async-start(bf16[2,128,512]{1,2,0:T(8,128)(2,1)} %copy.39), calls=%async_computation | async-start | bytes 524288 | tf_op jit(solution)/shard_map/all_to_all | solution.py:85
  106.6 33.1 %psum.7 = f32[4,128]{1,0:T(4,128)S(1)} all-reduce(f32[4,128]{1,0:T(4,128)S(1)} %get-tuple-element.15), channel_id=1, replica_groups=mesh['seq'=8,'head'=2,'dp'=2] {'seq','dp'}, use_global_device_ids=true, to_apply=%region_3.4 | all-reduce | flops 512 | bytes 4096 | tf_op jit(solution)/shard_map/psum | solution.py:97
  139.7 0.2 fusion.32
  139.9 0.0 collective-permute-done.14
  140.0 1.0 fusion.10
  140.9 1.3 collective-permute-start.15
  142.2 0.6 broadcast_multiply_fusion.2
  142.8 1.3 convolution_bitcast_fusion
  144.1 13.4 %collective-permute-done.15 = f32[4,128,128]{1,2,0:T(8,128)S(1)} collective-permute-done((f32[4,128,128]{1,2,0:T(8,128)S(1)}, f32[4,128,128]{1,2,0:T(8,128)S(1)}, u32[]{:S(2)}, u32[]{:S(2)}) %collective-permute-start.15) | collective-permute-done | bytes 262176 | tf_op jit(solution)/shard_map/ppermute | solution.py:14
  157.6 0.1 fusion.18
  157.6 0.4 fusion.6
  158.0 0.8 copy.52
  158.9 0.4 fusion.5
  159.3 0.8 copy.51
  160.2 0.0 all-to-all-done
  160.2 3.7 %fusion = bf16[1,128,2048]{2,1,0:T(8,128)(2,1)} fusion(bf16[128,1024]{0,1:T(8,128)(2,1)S(1)} %bitcast.79, bf16[1024,2048]{1,0:T(8,128)(2,1)} %all-gather.2.cloned.1.call-done), kind=kOutput, calls=%fused_computation.1 | convolution fusion | flops 537133056 | bytes 4980736 | tf_op jit(solution)/shard_map/dot_general | solution.py:86
  (18 shorter events, 0.2 us)
Async XLA Ops:
  7.2 30.9 %copy-start = (bf16[1,256,2048]{2,1,0:T(8,128)(2,1)S(1)}, bf16[1,256,2048]{2,1,0:T(8,128)(2,1)}, u32[]{:S(2)}) copy-start(bf16[1,256,2048]{2,1,0:T(8,128)(2,1)} %param.13) | copy-start | bytes 3145732
  7.2 20.5 %copy-start.2 = (bf16[1,256,512]{2,1,0:T(8,128)(2,1)S(1)}, bf16[1,256,512]{2,1,0:T(8,128)(2,1)}, u32[]{:S(2)}) copy-start(bf16[1,256,512]{2,1,0:T(8,128)(2,1)} %param.7) | copy-start | bytes 786436
  7.2 153.0 %all-gather.2.cloned.1.call-start = ((), (), s32[]{:S(2)}) async-start(), calls=%async_computation.1 | async-start | bytes 6291456 | tf_op jit(solution)/shard_map/all_gather | solution.py:88
  10.5 9.1 %collective-permute-start.4 = (f32[4,128,128]{2,1,0:T(8,128)S(1)}, f32[4,128,128]{2,1,0:T(8,128)S(1)}, u32[]{:S(2)}, u32[]{:S(2)}) collective-permute-start(f32[4,128,128]{2,1,0:T(8,128)S(1)} %get-tuple-element.19), channel_id=1, source_target_pairs={{0,4},{4,8},{8,12},{12,16},{16,20},{20,24},{24,28},{1,5},{5,9},{9,... | collective-permute-start | bytes 786440 | tf_op jit(solution)/shard_map/ppermute | solution.py:14
  19.5 15.3 %collective-permute-start.5 = (f32[4,128,128]{2,1,0:T(8,128)S(1)}, f32[4,128,128]{2,1,0:T(8,128)S(1)}, u32[]{:S(2)}, u32[]{:S(2)}) collective-permute-start(f32[4,128,128]{2,1,0:T(8,128)S(1)} %collective-permute-done.4), channel_id=1, source_target_pairs={{0,4},{4,8},{8,12},{12,16},{16,20},{20,24},{24,28},{1,5},{5,9},{9,... | collective-permute-start | bytes 786440 | tf_op jit(solution)/shard_map/ppermute | solution.py:14
  23.6 4.6 %collective-permute-start = (f32[1]{0:T(128)}, f32[1]{0:T(128)}, u32[]{:S(2)}, u32[]{:S(2)}) collective-permute-start(f32[1]{0:T(128)} %bitcast.1), channel_id=1, source_target_pairs={{0,4},{4,8},{8,12},{12,16},{16,20},{20,24},{24,28},{1,5},{5,9},{9,... | collective-permute-start | bytes 20 | tf_op jit(solution)/shard_map/ppermute | solution.py:14
  28.2 5.3 %collective-permute-start.1 = (f32[1]{0:T(128)}, f32[1]{0:T(128)}, u32[]{:S(2)}, u32[]{:S(2)}) collective-permute-start(f32[1]{0:T(128)} %collective-permute-done), channel_id=1, source_target_pairs={{0,4},{4,8},{8,12},{12,16},{16,20},{20,24},{24,28},{1,5},{5,9},{9,... | collective-permute-start | bytes 20 | tf_op jit(solution)/shard_map/ppermute | solution.py:14
  34.8 21.2 %copy-start.3 = (f32[4,128]{1,0:T(4,128)S(1)}, f32[4,128]{1,0:T(4,128)}, u32[]{:S(2)}) copy-start(f32[4,128]{1,0:T(4,128)} %param.11) | copy-start | bytes 6148
  34.8 11.7 %collective-permute-start.6 = (f32[4,128,128]{2,1,0:T(8,128)S(1)}, f32[4,128,128]{2,1,0:T(8,128)S(1)}, u32[]{:S(2)}, u32[]{:S(2)}) collective-permute-start(f32[4,128,128]{2,1,0:T(8,128)S(1)} %fusion.14), channel_id=1, source_target_pairs={{0,8},{4,12},{8,16},{12,20},{16,24},{20,28},{1,9},{5,13},{9,17},{1... | collective-permute-start | bytes 786440 | tf_op jit(solution)/shard_map/ppermute | solution.py:14
  42.0 3.9 %collective-permute-start.2 = (f32[1]{0:T(128)}, f32[1]{0:T(128)}, u32[]{:S(2)}, u32[]{:S(2)}) collective-permute-start(f32[1]{0:T(128)} %select_n.117), channel_id=1, source_target_pairs={{0,8},{4,12},{8,16},{12,20},{16,24},{20,28},{1,9},{5,13},{9,17},{1... | collective-permute-start | bytes 20 | tf_op jit(solution)/shard_map/ppermute | solution.py:14
  46.6 8.8 %collective-permute-start.7 = (f32[4,128,128]{2,1,0:T(8,128)S(1)}, f32[4,128,128]{2,1,0:T(8,128)S(1)}, u32[]{:S(2)}, u32[]{:S(2)}) collective-permute-start(f32[4,128,128]{2,1,0:T(8,128)S(1)} %fusion.13), channel_id=1, source_target_pairs={{0,16},{4,20},{8,24},{12,28},{1,17},{5,21},{9,25},{13,29},{2,18},{... | collective-permute-start | bytes 786440 | tf_op jit(solution)/shard_map/ppermute | solution.py:14
  52.1 2.1 %collective-permute-start.3 = (f32[1]{0:T(128)}, f32[1]{0:T(128)}, u32[]{:S(2)}, u32[]{:S(2)}) collective-permute-start(f32[1]{0:T(128)} %select_n.118), channel_id=1, source_target_pairs={{0,16},{4,20},{8,24},{12,28},{1,17},{5,21},{9,25},{13,29},{2,18},{... | collective-permute-start | bytes 20 | tf_op jit(solution)/shard_map/ppermute | solution.py:14
  57.4 33.4 %collective-permute-start.12 = (f32[4,128,128]{1,2,0:T(8,128)S(1)}, f32[4,128,128]{1,2,0:T(8,128)S(1)}, u32[]{:S(2)}, u32[]{:S(2)}) collective-permute-start(f32[4,128,128]{1,2,0:T(8,128)S(1)} %multiply_bitcast_fusion), channel_id=1, source_target_pairs={{4,0},{8,4},{12,8},{16,12},{20,16},{24,20},{28,24},{5,1},{9,5},{13... | collective-permute-start | bytes 786440 | tf_op jit(solution)/shard_map/ppermute | solution.py:14
  61.5 10.6 %collective-permute-start.8 = (f32[1]{0:T(128)}, f32[1]{0:T(128)}, u32[]{:S(2)}, u32[]{:S(2)}) collective-permute-start(f32[1]{0:T(128)} %bitcast.1), channel_id=1, source_target_pairs={{4,0},{8,4},{12,8},{16,12},{20,16},{24,20},{28,24},{5,1},{9,5},{13... | collective-permute-start | bytes 20 | tf_op jit(solution)/shard_map/ppermute | solution.py:14
  72.1 5.3 %collective-permute-start.9 = (f32[1]{0:T(128)}, f32[1]{0:T(128)}, u32[]{:S(2)}, u32[]{:S(2)}) collective-permute-start(f32[1]{0:T(128)} %collective-permute-done.8), channel_id=1, source_target_pairs={{4,0},{8,4},{12,8},{16,12},{20,16},{24,20},{28,24},{5,1},{9,5},{13... | collective-permute-start | bytes 20 | tf_op jit(solution)/shard_map/ppermute | solution.py:14
  78.7 4.8 %collective-permute-start.10 = (f32[1]{0:T(128)}, f32[1]{0:T(128)}, u32[]{:S(2)}, u32[]{:S(2)}) collective-permute-start(f32[1]{0:T(128)} %select_n.135), channel_id=1, source_target_pairs={{8,0},{12,4},{16,8},{20,12},{24,16},{28,20},{9,1},{13,5},{17,9},{2... | collective-permute-start | bytes 20 | tf_op jit(solution)/shard_map/ppermute | solution.py:14
  84.1 5.4 %collective-permute-start.11 = (f32[1]{0:T(128)}, f32[1]{0:T(128)}, u32[]{:S(2)}, u32[]{:S(2)}) collective-permute-start(f32[1]{0:T(128)} %select_n.136), channel_id=1, source_target_pairs={{16,0},{20,4},{24,8},{28,12},{17,1},{21,5},{25,9},{29,13},{18,2},{... | collective-permute-start | bytes 20 | tf_op jit(solution)/shard_map/ppermute | solution.py:14
  90.8 8.0 %collective-permute-start.13 = (f32[4,128,128]{1,2,0:T(8,128)S(1)}, f32[4,128,128]{1,2,0:T(8,128)S(1)}, u32[]{:S(2)}, u32[]{:S(2)}) collective-permute-start(f32[4,128,128]{1,2,0:T(8,128)S(1)} %collective-permute-done.12), channel_id=1, source_target_pairs={{4,0},{8,4},{12,8},{16,12},{20,16},{24,20},{28,24},{5,1},{9,5},{13... | collective-permute-start | bytes 786440 | tf_op jit(solution)/shard_map/ppermute | solution.py:14
  93.1 7.4 %copy-start.1 = (bf16[4,256,256]{2,1,0:T(8,128)(2,1)}, bf16[4,256,256]{2,1,0:T(8,128)(2,1)S(1)}, u32[]{:S(2)}) copy-start(bf16[4,256,256]{2,1,0:T(8,128)(2,1)S(1)} %fusion.2) | copy-start | bytes 1572868
  98.9 41.1 %collective-permute-start.14 = (f32[4,128,128]{1,2,0:T(8,128)S(1)}, f32[4,128,128]{1,2,0:T(8,128)}, u32[]{:S(2)}, u32[]{:S(2)}) collective-permute-start(f32[4,128,128]{1,2,0:T(8,128)S(1)} %fusion.11), channel_id=1, source_target_pairs={{8,0},{12,4},{16,8},{20,12},{24,16},{28,20},{9,1},{13,5},{17,9},{2... | collective-permute-start | bytes 786440 | tf_op jit(solution)/shard_map/ppermute | solution.py:14
  103.1 57.0 %all-to-all-start = ((bf16[2,128,512]{1,2,0:T(8,128)(2,1)}), bf16[2,128,512]{1,2,0:T(8,128)(2,1)S(1)}, u32[]{:S(2)}, u32[]{:S(2)}) async-start(bf16[2,128,512]{1,2,0:T(8,128)(2,1)} %copy.39), calls=%async_computation | async-start | bytes 524288 | tf_op jit(solution)/shard_map/all_to_all | solution.py:85
  140.9 16.6 %collective-permute-start.15 = (f32[4,128,128]{1,2,0:T(8,128)S(1)}, f32[4,128,128]{1,2,0:T(8,128)S(1)}, u32[]{:S(2)}, u32[]{:S(2)}) collective-permute-start(f32[4,128,128]{1,2,0:T(8,128)S(1)} %fusion.10), channel_id=1, source_target_pairs={{16,0},{20,4},{24,8},{28,12},{17,1},{21,5},{25,9},{29,13},{18,2},{... | collective-permute-start | bytes 786440 | tf_op jit(solution)/shard_map/ppermute | solution.py:14
Sparse Core Ops, SparseCore 0:
  27.8 57.8 all-gather.1
where the time goes:
time: 172 us; the launch traced here: 171 us
  starting transfers between devices  49.1 us (29%)
  waiting for transfers between devices  41.2 us (24%)
  blocking collectives  33.1 us (19%)
  between operations  26.5 us (15%)
  matrix products  11.2 us (7%)
  local copies, waits for them, and re-layouts  6.59 us (4%)
  other arithmetic  2.95 us (2%)
    ppermute x16, starting transfers between devices, shifted(): return lax.ppermute(block, axis, route)  45.6 us
    ppermute x16, waiting for transfers between devices, shifted(): return lax.ppermute(block, axis, route)  41.2 us
    psum x1, blocking collectives, on_device(): gain_grad = lax.psum(gain_part, ('seq', 'dp')) / math.sqrt(total_tokens)  33.1 us
    dot_general x1, matrix products, on_device(): jnp.dot(exchanged, lax.all_gather(w_out, 'head', axis=0, tiled=True), pre...  3.72 us
  transfers between devices with their start and end apart: 18, of which 9 were waited for; matrix products, arithmetic and copies ran while one was open for 8% of the time, Pallas kernels for 0%

commit v1 on v0

--- a/solution.py
+++ b/solution.py
@@ -94,7 +94,7 @@
     ).reshape(blocks)
     gain_part = jnp.sum(grad_normed * unit_rows, axis=(0, 1))
     total_tokens = seq_size * lax.axis_size("dp") * token_count
-    gain_grad = lax.psum(gain_part, ("seq", "dp")) / math.sqrt(total_tokens)
+    gain_grad = lax.psum(lax.psum(gain_part, "dp"), "seq") / math.sqrt(total_tokens)
     scaled = grad_normed * head_gain
     grad_attended = inv_rms * (
         scaled - unit_rows * jnp.mean(scaled * unit_rows, axis=-1, keepdims=True)

time: 172 us -> 164 us (0.953)
  the two profiles are of different devices: /device:TPU:7 before, /device:TPU:0 now
where the time goes in v1:
time: 164 us; the launch traced here: 163 us
  starting transfers between devices  52.5 us (32%)
  waiting for transfers between devices  39.4 us (24%)
  between operations  25.6 us (16%)
  blocking collectives  25.5 us (16%)
  matrix products  10.9 us (7%)
  local copies, waits for them, and re-layouts  6.6 us (4%)
  other arithmetic  2.95 us (2%)
    ppermute x16, starting transfers between devices, shifted(): return lax.ppermute(block, axis, route)  49 us
    ppermute x16, waiting for transfers between devices, shifted(): return lax.ppermute(block, axis, route)  39.4 us
    psum x1, blocking collectives, on_device(): lax.psum(lax.psum(gain_part, 'dp'), 'seq') / math.sqrt(total_tokens)  23.1 us
    dot_general x1, matrix products, on_device(): jnp.dot(exchanged, lax.all_gather(w_out, 'head', axis=0, tiled=True), pre...  3.73 us
    all_to_all x1, starting transfers between devices, on_device(): lax.all_to_all(normed_rows, 'head', split_axis=0, concat_axis=1, tiled=True)  3.44 us
  transfers between devices with their start and end apart: 18, of which 8 were waited for; matrix products, arithmetic and copies ran while one was open for 8% of the time, Pallas kernels for 0%

profile of v1, /device:TPU:0, one launch (start us, length us, event | category | flops | bytes accessed | tf_op | source)
XLA Modules:
  0.0 163.5 jit_solution(10275549119583446655)
XLA Ops:
  7.2 0.0 copy-start
  7.2 0.0 all-gather.2.cloned.1.call-start
  8.0 1.0 reshape.195
  9.0 0.2 copy.35
  9.2 1.0 reshape.196
  10.2 0.2 broadcast_multiply_fusion
  10.5 4.9 %collective-permute-start.4 = (f32[4,128,128]{2,1,0:T(8,128)S(1)}, f32[4,128,128]{2,1,0:T(8,128)S(1)}, u32[]{:S(2)}, u32[]{:S(2)}) collective-permute-start(f32[4,128,128]{2,1,0:T(8,128)S(1)} %get-tuple-element.19), channel_id=1, source_target_pairs={{0,4},{4,8},{8,12},{12,16},{16,20},{20,24},{24,28},{1,5},{5,9},{9,... | collective-permute-start | bytes 786440 | tf_op jit(solution)/shard_map/ppermute | solution.py:14
  15.3 5.5 %collective-permute-done.4 = f32[4,128,128]{2,1,0:T(8,128)S(1)} collective-permute-done((f32[4,128,128]{2,1,0:T(8,128)S(1)}, f32[4,128,128]{2,1,0:T(8,128)S(1)}, u32[]{:S(2)}, u32[]{:S(2)}) %collective-permute-start.4) | collective-permute-done | bytes 262176 | tf_op jit(solution)/shard_map/ppermute | solution.py:14
  20.9 4.4 %collective-permute-start.5 = (f32[4,128,128]{2,1,0:T(8,128)S(1)}, f32[4,128,128]{2,1,0:T(8,128)S(1)}, u32[]{:S(2)}, u32[]{:S(2)}) collective-permute-start(f32[4,128,128]{2,1,0:T(8,128)S(1)} %collective-permute-done.4), channel_id=1, source_target_pairs={{0,4},{4,8},{8,12},{12,16},{16,20},{20,24},{24,28},{1,5},{5,9},{9,... | collective-permute-start | bytes 786440 | tf_op jit(solution)/shard_map/ppermute | solution.py:14
  25.2 5.6 %collective-permute-start = (f32[1]{0:T(128)}, f32[1]{0:T(128)}, u32[]{:S(2)}, u32[]{:S(2)}) collective-permute-start(f32[1]{0:T(128)} %bitcast.1), channel_id=1, source_target_pairs={{0,4},{4,8},{8,12},{12,16},{16,20},{20,24},{24,28},{1,5},{5,9},{9,... | collective-permute-start | bytes 20 | tf_op jit(solution)/shard_map/ppermute | solution.py:14
  30.9 0.0 all-gather.2.cloned.1.call-update
  30.9 0.1 reshape.194
  31.0 4.6 %collective-permute-start.1 = (f32[1]{0:T(128)}, f32[1]{0:T(128)}, u32[]{:S(2)}, u32[]{:S(2)}) collective-permute-start(f32[1]{0:T(128)} %collective-permute-done), channel_id=1, source_target_pairs={{0,4},{4,8},{8,12},{12,16},{16,20},{20,24},{24,28},{1,5},{5,9},{9,... | collective-permute-start | bytes 20 | tf_op jit(solution)/shard_map/ppermute | solution.py:14
  36.2 0.4 collective-permute-done.1
  37.7 0.0 collective-permute-done.5
  37.8 0.0 copy-start.3
  37.8 6.4 %collective-permute-start.6 = (f32[4,128,128]{2,1,0:T(8,128)S(1)}, f32[4,128,128]{2,1,0:T(8,128)S(1)}, u32[]{:S(2)}, u32[]{:S(2)}) collective-permute-start(f32[4,128,128]{2,1,0:T(8,128)S(1)} %fusion.14), channel_id=1, source_target_pairs={{0,8},{4,12},{8,16},{12,20},{16,24},{20,28},{1,9},{5,13},{9,17},{1... | collective-permute-start | bytes 786440 | tf_op jit(solution)/shard_map/ppermute | solution.py:14
  44.2 2.3 %fusion.7 = f32[256,512]{0,1:T(8,128)S(1)} fusion(bf16[512,2048]{1,0:T(8,128)(2,1)} %param.12, bf16[1,256,2048]{2,1,0:T(8,128)(2,1)S(1)} %copy-done), kind=kOutput, calls=%fused_computation.17 | convolution fusion | flops 536870912 | bytes 3670016 | tf_op jit(solution)/shard_map/tm,fm->tf/dot_general | solution.py:92
  47.7 4.9 %collective-permute-start.2 = (f32[1]{0:T(128)}, f32[1]{0:T(128)}, u32[]{:S(2)}, u32[]{:S(2)}) collective-permute-start(f32[1]{0:T(128)} %select_n.117), channel_id=1, source_target_pairs={{0,8},{4,12},{8,16},{12,20},{16,24},{20,28},{1,9},{5,13},{9,17},{1... | collective-permute-start | bytes 20 | tf_op jit(solution)/shard_map/ppermute | solution.py:14
  53.1 0.0 collective-permute-done.6
  53.2 5.2 %collective-permute-start.7 = (f32[4,128,128]{2,1,0:T(8,128)S(1)}, f32[4,128,128]{2,1,0:T(8,128)S(1)}, u32[]{:S(2)}, u32[]{:S(2)}) collective-permute-start(f32[4,128,128]{2,1,0:T(8,128)S(1)} %fusion.13), channel_id=1, source_target_pairs={{0,16},{4,20},{8,24},{12,28},{1,17},{5,21},{9,25},{13,29},{2,18},{... | collective-permute-start | bytes 786440 | tf_op jit(solution)/shard_map/ppermute | solution.py:14
  58.3 0.3 fusion.1
  58.7 0.3 convolution_bitcast_fusion.2
  59.5 2.8 %collective-permute-start.3 = (f32[1]{0:T(128)}, f32[1]{0:T(128)}, u32[]{:S(2)}, u32[]{:S(2)}) collective-permute-start(f32[1]{0:T(128)} %select_n.118), channel_id=1, source_target_pairs={{0,16},{4,20},{8,24},{12,28},{1,17},{5,21},{9,25},{13,29},{2,18},{... | collective-permute-start | bytes 20 | tf_op jit(solution)/shard_map/ppermute | solution.py:14
  63.4 0.1 fusion.16
  63.5 0.5 multiply_reduce_fusion.2
  64.0 0.2 multiply_reduce_fusion
  64.2 0.9 fusion.19
  65.1 0.2 fusion.28
  65.3 1.3 collective-permute-start.12
  66.6 1.3 collective-permute-start.8
  67.9 5.8 %collective-permute-done.8 = f32[1]{0:T(128)} collective-permute-done((f32[1]{0:T(128)}, f32[1]{0:T(128)}, u32[]{:S(2)}, u32[]{:S(2)}) %collective-permute-start.8) | collective-permute-done | bytes 36 | tf_op jit(solution)/shard_map/ppermute | solution.py:14
  73.8 1.3 collective-permute-start.9
  75.7 4.5 %collective-permute-done.9 = f32[1]{0:T(128)} collective-permute-done((f32[1]{0:T(128)}, f32[1]{0:T(128)}, u32[]{:S(2)}, u32[]{:S(2)}) %collective-permute-start.9) | collective-permute-done | bytes 36 | tf_op jit(solution)/shard_map/ppermute | solution.py:14
  81.3 1.3 collective-permute-start.10
  83.8 3.5 %collective-permute-done.10 = f32[1]{0:T(128)} collective-permute-done((f32[1]{0:T(128)}, f32[1]{0:T(128)}, u32[]{:S(2)}, u32[]{:S(2)}) %collective-permute-start.10) | collective-permute-done | bytes 36 | tf_op jit(solution)/shard_map/ppermute | solution.py:14
  87.9 1.3 collective-permute-start.11
  89.8 4.5 %collective-permute-done.11 = f32[1]{0:T(128)} collective-permute-done((f32[1]{0:T(128)}, f32[1]{0:T(128)}, u32[]{:S(2)}, u32[]{:S(2)}) %collective-permute-start.11) | collective-permute-done | bytes 36 | tf_op jit(solution)/shard_map/ppermute | solution.py:14
  95.5 1.3 collective-permute-start.13
  96.8 0.3 fusion.2
  97.1 0.0 copy-start.1
  97.1 0.3 convolution_bitcast_fusion.1
  97.5 7.1 %collective-permute-done.13 = f32[4,128,128]{1,2,0:T(8,128)S(1)} collective-permute-done((f32[4,128,128]{1,2,0:T(8,128)S(1)}, f32[4,128,128]{1,2,0:T(8,128)S(1)}, u32[]{:S(2)}, u32[]{:S(2)}) %collective-permute-start.13) | collective-permute-done | bytes 262176 | tf_op jit(solution)/shard_map/ppermute | solution.py:14
  104.6 1.3 collective-permute-start.14
  105.9 0.4 fusion.4
  106.3 0.8 copy.50
  107.1 1.0 all_to_all.14
  108.1 0.7 copy.39
  108.9 3.4 %all-to-all-start = ((bf16[2,128,512]{1,2,0:T(8,128)(2,1)}), bf16[2,128,512]{1,2,0:T(8,128)(2,1)S(1)}, u32[]{:S(2)}, u32[]{:S(2)}) async-start(bf16[2,128,512]{1,2,0:T(8,128)(2,1)} %copy.39), calls=%async_computation | async-start | bytes 524288 | tf_op jit(solution)/shard_map/all_to_all | solution.py:85
  112.3 2.5 %psum.14 = f32[4,128]{1,0:T(4,128)S(1)} all-reduce(f32[4,128]{1,0:T(4,128)S(1)} %get-tuple-element.15), channel_id=1, replica_groups=mesh['seq'=8,'head'=2,'dp'=2] {'dp'}, use_global_device_ids=true, to_apply=%region_3.4 | all-reduce | flops 512 | bytes 4096 | tf_op jit(solution)/shard_map/psum | solution.py:97
  114.8 23.1 %psum.15 = f32[4,128]{1,0:T(4,128)S(1)} all-reduce(f32[4,128]{1,0:T(4,128)S(1)} %psum.14), channel_id=1, replica_groups=mesh['seq'=8,'head'=2,'dp'=2] {'seq'}, use_global_device_ids=true, to_apply=%region_4.5 | all-reduce | flops 512 | bytes 4096 | tf_op jit(solution)/shard_map/psum | solution.py:97
  137.9 0.2 fusion.32
  138.1 1.0 fusion.10
  139.1 1.3 collective-permute-start.15
  140.4 0.6 broadcast_multiply_fusion.2
  141.0 1.3 convolution_bitcast_fusion
  142.3 8.0 %collective-permute-done.15 = f32[4,128,128]{1,2,0:T(8,128)S(1)} collective-permute-done((f32[4,128,128]{1,2,0:T(8,128)S(1)}, f32[4,128,128]{1,2,0:T(8,128)S(1)}, u32[]{:S(2)}, u32[]{:S(2)}) %collective-permute-start.15) | collective-permute-done | bytes 262176 | tf_op jit(solution)/shard_map/ppermute | solution.py:14
  150.3 0.1 fusion.18
  150.4 0.4 fusion.6
  150.8 0.8 copy.52
  151.6 0.4 fusion.5
  152.0 0.8 copy.51
  152.9 0.0 all-to-all-done
  152.9 3.7 %fusion = bf16[1,128,2048]{2,1,0:T(8,128)(2,1)} fusion(bf16[128,1024]{0,1:T(8,128)(2,1)S(1)} %bitcast.79, bf16[1024,2048]{1,0:T(8,128)(2,1)} %all-gather.2.cloned.1.call-done), kind=kOutput, calls=%fused_computation.1 | convolution fusion | flops 537133056 | bytes 4980736 | tf_op jit(solution)/shard_map/dot_general | solution.py:86
  (19 shorter events, 0.2 us)
Async XLA Ops:
  7.2 37.0 %copy-start = (bf16[1,256,2048]{2,1,0:T(8,128)(2,1)S(1)}, bf16[1,256,2048]{2,1,0:T(8,128)(2,1)}, u32[]{:S(2)}) copy-start(bf16[1,256,2048]{2,1,0:T(8,128)(2,1)} %param.13) | copy-start | bytes 3145732
  7.2 23.7 %copy-start.2 = (bf16[1,256,512]{2,1,0:T(8,128)(2,1)S(1)}, bf16[1,256,512]{2,1,0:T(8,128)(2,1)}, u32[]{:S(2)}) copy-start(bf16[1,256,512]{2,1,0:T(8,128)(2,1)} %param.7) | copy-start | bytes 786436
  7.2 145.7 %all-gather.2.cloned.1.call-start = ((), (), s32[]{:S(2)}) async-start(), calls=%async_computation.1 | async-start | bytes 6291456 | tf_op jit(solution)/shard_map/all_gather | solution.py:88
  10.5 10.4 %collective-permute-start.4 = (f32[4,128,128]{2,1,0:T(8,128)S(1)}, f32[4,128,128]{2,1,0:T(8,128)S(1)}, u32[]{:S(2)}, u32[]{:S(2)}) collective-permute-start(f32[4,128,128]{2,1,0:T(8,128)S(1)} %get-tuple-element.19), channel_id=1, source_target_pairs={{0,4},{4,8},{8,12},{12,16},{16,20},{20,24},{24,28},{1,5},{5,9},{9,... | collective-permute-start | bytes 786440 | tf_op jit(solution)/shard_map/ppermute | solution.py:14
  20.9 16.9 %collective-permute-start.5 = (f32[4,128,128]{2,1,0:T(8,128)S(1)}, f32[4,128,128]{2,1,0:T(8,128)S(1)}, u32[]{:S(2)}, u32[]{:S(2)}) collective-permute-start(f32[4,128,128]{2,1,0:T(8,128)S(1)} %collective-permute-done.4), channel_id=1, source_target_pairs={{0,4},{4,8},{8,12},{12,16},{16,20},{20,24},{24,28},{1,5},{5,9},{9,... | collective-permute-start | bytes 786440 | tf_op jit(solution)/shard_map/ppermute | solution.py:14
  25.2 5.8 %collective-permute-start = (f32[1]{0:T(128)}, f32[1]{0:T(128)}, u32[]{:S(2)}, u32[]{:S(2)}) collective-permute-start(f32[1]{0:T(128)} %bitcast.1), channel_id=1, source_target_pairs={{0,4},{4,8},{8,12},{12,16},{16,20},{20,24},{24,28},{1,5},{5,9},{9,... | collective-permute-start | bytes 20 | tf_op jit(solution)/shard_map/ppermute | solution.py:14
  31.0 5.6 %collective-permute-start.1 = (f32[1]{0:T(128)}, f32[1]{0:T(128)}, u32[]{:S(2)}, u32[]{:S(2)}) collective-permute-start(f32[1]{0:T(128)} %collective-permute-done), channel_id=1, source_target_pairs={{0,4},{4,8},{8,12},{12,16},{16,20},{20,24},{24,28},{1,5},{5,9},{9,... | collective-permute-start | bytes 20 | tf_op jit(solution)/shard_map/ppermute | solution.py:14
  37.8 26.2 %copy-start.3 = (f32[4,128]{1,0:T(4,128)S(1)}, f32[4,128]{1,0:T(4,128)}, u32[]{:S(2)}) copy-start(f32[4,128]{1,0:T(4,128)} %param.11) | copy-start | bytes 6148
  37.8 15.3 %collective-permute-start.6 = (f32[4,128,128]{2,1,0:T(8,128)S(1)}, f32[4,128,128]{2,1,0:T(8,128)S(1)}, u32[]{:S(2)}, u32[]{:S(2)}) collective-permute-start(f32[4,128,128]{2,1,0:T(8,128)S(1)} %fusion.14), channel_id=1, source_target_pairs={{0,8},{4,12},{8,16},{12,20},{16,24},{20,28},{1,9},{5,13},{9,17},{1... | collective-permute-start | bytes 786440 | tf_op jit(solution)/shard_map/ppermute | solution.py:14
  47.7 4.9 %collective-permute-start.2 = (f32[1]{0:T(128)}, f32[1]{0:T(128)}, u32[]{:S(2)}, u32[]{:S(2)}) collective-permute-start(f32[1]{0:T(128)} %select_n.117), channel_id=1, source_target_pairs={{0,8},{4,12},{8,16},{12,20},{16,24},{20,28},{1,9},{5,13},{9,17},{1... | collective-permute-start | bytes 20 | tf_op jit(solution)/shard_map/ppermute | solution.py:14
  53.2 10.2 %collective-permute-start.7 = (f32[4,128,128]{2,1,0:T(8,128)S(1)}, f32[4,128,128]{2,1,0:T(8,128)S(1)}, u32[]{:S(2)}, u32[]{:S(2)}) collective-permute-start(f32[4,128,128]{2,1,0:T(8,128)S(1)} %fusion.13), channel_id=1, source_target_pairs={{0,16},{4,20},{8,24},{12,28},{1,17},{5,21},{9,25},{13,29},{2,18},{... | collective-permute-start | bytes 786440 | tf_op jit(solution)/shard_map/ppermute | solution.py:14
  59.5 2.8 %collective-permute-start.3 = (f32[1]{0:T(128)}, f32[1]{0:T(128)}, u32[]{:S(2)}, u32[]{:S(2)}) collective-permute-start(f32[1]{0:T(128)} %select_n.118), channel_id=1, source_target_pairs={{0,16},{4,20},{8,24},{12,28},{1,17},{5,21},{9,25},{13,29},{2,18},{... | collective-permute-start | bytes 20 | tf_op jit(solution)/shard_map/ppermute | solution.py:14
  65.3 30.2 %collective-permute-start.12 = (f32[4,128,128]{1,2,0:T(8,128)S(1)}, f32[4,128,128]{1,2,0:T(8,128)S(1)}, u32[]{:S(2)}, u32[]{:S(2)}) collective-permute-start(f32[4,128,128]{1,2,0:T(8,128)S(1)} %multiply_bitcast_fusion), channel_id=1, source_target_pairs={{4,0},{8,4},{12,8},{16,12},{20,16},{24,20},{28,24},{5,1},{9,5},{13... | collective-permute-start | bytes 786440 | tf_op jit(solution)/shard_map/ppermute | solution.py:14
  66.6 7.1 %collective-permute-start.8 = (f32[1]{0:T(128)}, f32[1]{0:T(128)}, u32[]{:S(2)}, u32[]{:S(2)}) collective-permute-start(f32[1]{0:T(128)} %bitcast.1), channel_id=1, source_target_pairs={{4,0},{8,4},{12,8},{16,12},{20,16},{24,20},{28,24},{5,1},{9,5},{13... | collective-permute-start | bytes 20 | tf_op jit(solution)/shard_map/ppermute | solution.py:14
  73.8 6.4 %collective-permute-start.9 = (f32[1]{0:T(128)}, f32[1]{0:T(128)}, u32[]{:S(2)}, u32[]{:S(2)}) collective-permute-start(f32[1]{0:T(128)} %collective-permute-done.8), channel_id=1, source_target_pairs={{4,0},{8,4},{12,8},{16,12},{20,16},{24,20},{28,24},{5,1},{9,5},{13... | collective-permute-start | bytes 20 | tf_op jit(solution)/shard_map/ppermute | solution.py:14
  81.3 5.9 %collective-permute-start.10 = (f32[1]{0:T(128)}, f32[1]{0:T(128)}, u32[]{:S(2)}, u32[]{:S(2)}) collective-permute-start(f32[1]{0:T(128)} %select_n.135), channel_id=1, source_target_pairs={{8,0},{12,4},{16,8},{20,12},{24,16},{28,20},{9,1},{13,5},{17,9},{2... | collective-permute-start | bytes 20 | tf_op jit(solution)/shard_map/ppermute | solution.py:14
  87.9 6.4 %collective-permute-start.11 = (f32[1]{0:T(128)}, f32[1]{0:T(128)}, u32[]{:S(2)}, u32[]{:S(2)}) collective-permute-start(f32[1]{0:T(128)} %select_n.136), channel_id=1, source_target_pairs={{16,0},{20,4},{24,8},{28,12},{17,1},{21,5},{25,9},{29,13},{18,2},{... | collective-permute-start | bytes 20 | tf_op jit(solution)/shard_map/ppermute | solution.py:14
  95.5 9.1 %collective-permute-start.13 = (f32[4,128,128]{1,2,0:T(8,128)S(1)}, f32[4,128,128]{1,2,0:T(8,128)S(1)}, u32[]{:S(2)}, u32[]{:S(2)}) collective-permute-start(f32[4,128,128]{1,2,0:T(8,128)S(1)} %collective-permute-done.12), channel_id=1, source_target_pairs={{4,0},{8,4},{12,8},{16,12},{20,16},{24,20},{28,24},{5,1},{9,5},{13... | collective-permute-start | bytes 786440 | tf_op jit(solution)/shard_map/ppermute | solution.py:14
  97.1 9.1 %copy-start.1 = (bf16[4,256,256]{2,1,0:T(8,128)(2,1)}, bf16[4,256,256]{2,1,0:T(8,128)(2,1)S(1)}, u32[]{:S(2)}) copy-start(bf16[4,256,256]{2,1,0:T(8,128)(2,1)S(1)} %fusion.2) | copy-start | bytes 1572868
  104.6 33.5 %collective-permute-start.14 = (f32[4,128,128]{1,2,0:T(8,128)S(1)}, f32[4,128,128]{1,2,0:T(8,128)}, u32[]{:S(2)}, u32[]{:S(2)}) collective-permute-start(f32[4,128,128]{1,2,0:T(8,128)S(1)} %fusion.11), channel_id=1, source_target_pairs={{8,0},{12,4},{16,8},{20,12},{24,16},{28,20},{9,1},{13,5},{17,9},{2... | collective-permute-start | bytes 786440 | tf_op jit(solution)/shard_map/ppermute | solution.py:14
  108.9 44.0 %all-to-all-start = ((bf16[2,128,512]{1,2,0:T(8,128)(2,1)}), bf16[2,128,512]{1,2,0:T(8,128)(2,1)S(1)}, u32[]{:S(2)}, u32[]{:S(2)}) async-start(bf16[2,128,512]{1,2,0:T(8,128)(2,1)} %copy.39), calls=%async_computation | async-start | bytes 524288 | tf_op jit(solution)/shard_map/all_to_all | solution.py:85
  139.1 11.2 %collective-permute-start.15 = (f32[4,128,128]{1,2,0:T(8,128)S(1)}, f32[4,128,128]{1,2,0:T(8,128)S(1)}, u32[]{:S(2)}, u32[]{:S(2)}) collective-permute-start(f32[4,128,128]{1,2,0:T(8,128)S(1)} %fusion.10), channel_id=1, source_target_pairs={{16,0},{20,4},{24,8},{28,12},{17,1},{21,5},{25,9},{29,13},{18,2},{... | collective-permute-start | bytes 786440 | tf_op jit(solution)/shard_map/ppermute | solution.py:14
Sparse Core Ops, SparseCore 0:
  31.0 57.0 all-gather.1
